TPU v7x, 32 devices: a whole 2x2x4 slice. The times are simulated.
32 devices in a mesh: seq: 4 (over z), exp: 2 (over core), hid: 4 (over y, x).
Axes of the slice: x: 2, y: 2, z: 4, core: 2. Of those that a mesh axis runs over, the one named last changes fastest.
Arguments:
- tokens: bfloat16 [512, 6144], P('seq'), may hold values from -6 to 6
- out_grad: bfloat16 [512, 6144], P('seq'), may hold values from -3 to 3
- expert_ids: int32 [512, 2], P('seq'), may hold values from 0 to 7, as said below
- gate_probs: float32 [512, 2], P('seq'), may hold values from 0.1 to 1
- w_gate: bfloat16 [2, 6144, 16384], P('exp', None, ('seq', 'hid')), may hold values from -0.078125 to 0.078125
- w_up: bfloat16 [2, 6144, 16384], P('exp', None, ('seq', 'hid')), may hold values from -0.078125 to 0.078125
- w_down: bfloat16 [2, 16384, 6144], P('exp', ('seq', 'hid')), may hold values from -0.046875 to 0.046875
Outputs:
- d_w_gate: bfloat16 [2, 6144, 16384], P('exp', None, ('seq', 'hid'))
- d_w_up: bfloat16 [2, 6144, 16384], P('exp', None, ('seq', 'hid'))
- d_w_down: bfloat16 [2, 16384, 6144], P('exp', ('seq', 'hid'))
- d_tokens: float32 [512, 6144], P('seq', 'hid')
- d_gates: float32 [512, 2], P('seq')
Inputs may be any that keep to these rules, and one draw needn't show every extreme that they name: `expert_ids`: in each block of 128 rows (the tokens of one index of seq) the two ids of a row differ and no expert is named more than 40 times; each expert below 2 is named 40 // 2 to 40 times in a block, exactly 40 times in the first block.
All inputs are finite; a program needn't handle non-finite values.
Results may differ from a plain program's by a relative error of at most 0.015.
Values may be sent and summed in bfloat16 or wider, within the bound.
No kernel may reach another device: no remote copies, remote signals or barrier semaphores. Data moves between devices by JAX's collectives and lax.ppermute only.
A program may use at most 192 MiB of HBM per device.

v0:
```python
import jax
import jax.numpy as jnp
from jax import lax
from jax.sharding import PartitionSpec as P


def on_device(tokens, out_grad, expert_ids, gate_probs, w_gate, w_up, w_down):
    expert = lax.axis_index("exp")
    tok_rows = tokens.shape[0]
    model_width = tokens.shape[1]
    capacity = 5 * tok_rows // 16
    seq_count = lax.axis_size("seq")
    hid_count = lax.axis_size("hid")
    piece_width = model_width // hid_count
    hidden_local = w_gate.shape[2]
    chosen = (expert_ids == expert).astype(jnp.int32)
    slot_index = (jnp.cumsum(chosen.reshape(-1)) - 1).reshape(tok_rows, 2)
    columns = jnp.arange(capacity, dtype=jnp.int32)
    pick_table = (
        (chosen[:, :, None] == 1) & (slot_index[:, :, None] == columns[None, None, :])
    ).astype(jnp.float32)
    select_rows = jnp.sum(pick_table, axis=1)
    select_half = select_rows.astype(jnp.bfloat16)
    contract_rows = (((0,), (0,)), ((), ()))
    token_slots = lax.dot_general(
        select_half, tokens, contract_rows, preferred_element_type=jnp.float32
    ).astype(jnp.bfloat16)
    grad_slots = lax.dot_general(
        select_half, out_grad, contract_rows, preferred_element_type=jnp.float32
    ).astype(jnp.bfloat16)
    weight_slots = jnp.sum(pick_table * gate_probs[:, :, None], axis=(0, 1))
    rows_e, grads_e, weight_e = (
        lax.all_gather(token_slots, "seq", axis=0, tiled=True),
        lax.all_gather(grad_slots, "seq", axis=0, tiled=True),
        lax.all_gather(weight_slots.astype(jnp.bfloat16), "seq", axis=0, tiled=True).astype(
            weight_slots.dtype
        ),
    )
    gate_mat = w_gate[0]
    up_mat = w_up[0]
    down_mat = w_down[0]
    gate_pre = jnp.dot(rows_e, gate_mat, preferred_element_type=jnp.float32)
    up_pre = jnp.dot(rows_e, up_mat, preferred_element_type=jnp.float32)
    sig_gate = jax.nn.sigmoid(gate_pre)
    activated = gate_pre * sig_gate
    hidden = (activated * up_pre).astype(jnp.bfloat16)
    back_hidden = lax.dot_general(
        grads_e, down_mat, (((1,), (1,)), ((), ())), preferred_element_type=jnp.float32
    )
    slot_part = jnp.sum(hidden.astype(jnp.float32) * back_hidden, axis=1)
    weighted = (weight_e[:, None] * hidden.astype(jnp.float32)).astype(jnp.bfloat16)
    grad_down = lax.dot_general(
        weighted, grads_e, contract_rows, preferred_element_type=jnp.float32
    ).astype(jnp.bfloat16)
    scaled_back = weight_e[:, None] * back_hidden
    d_gate = (scaled_back * up_pre * (sig_gate * (1.0 + gate_pre * (1.0 - sig_gate)))).astype(
        jnp.bfloat16
    )
    d_up = (scaled_back * activated).astype(jnp.bfloat16)
    grad_gate = lax.dot_general(
        rows_e, d_gate, contract_rows, preferred_element_type=jnp.float32
    ).astype(jnp.bfloat16)
    grad_up = lax.dot_general(
        rows_e, d_up, contract_rows, preferred_element_type=jnp.float32
    ).astype(jnp.bfloat16)
    gate_blocks = d_gate.reshape(seq_count, capacity, hidden_local)
    up_blocks = d_up.reshape(seq_count, capacity, hidden_local)
    partials = jnp.einsum(
        "sqf,hcf->shqc",
        gate_blocks,
        gate_mat.reshape(hid_count, piece_width, hidden_local),
        preferred_element_type=jnp.float32,
    )
    partials = partials + jnp.einsum(
        "sqf,hcf->shqc",
        up_blocks,
        up_mat.reshape(hid_count, piece_width, hidden_local),
        preferred_element_type=jnp.float32,
    )
    slot_terms = jnp.broadcast_to(
        slot_part.reshape(seq_count, 1, capacity), (seq_count, hid_count, capacity)
    )
    flat_parts = partials.reshape(seq_count * hid_count, capacity, piece_width)
    flat_slots = slot_terms.reshape(seq_count * hid_count, capacity)
    partials, slot_terms = (
        lax.psum_scatter(flat_parts, ("seq", "hid"), scatter_dimension=0, tiled=True),
        lax.psum_scatter(flat_slots, ("seq", "hid"), scatter_dimension=0, tiled=True),
    )
    own_rows = partials.reshape(capacity, piece_width)
    slot_grad = slot_terms.reshape(capacity)
    token_part = jnp.dot(
        select_rows, own_rows, precision=lax.Precision.HIGHEST, preferred_element_type=jnp.float32
    )
    gate_part = jnp.sum(pick_table * slot_grad[None, None, :], axis=2)
    token_sum, gate_sum = (
        lax.psum(token_part.astype(jnp.bfloat16), "exp").astype(jnp.float32),
        lax.psum(gate_part.astype(jnp.bfloat16), "exp").astype(jnp.float32),
    )
    return (grad_gate[None], grad_up[None], grad_down[None], token_sum, gate_sum)


def solution(mesh):
    return jax.shard_map(
        on_device,
        mesh=mesh,
        in_specs=(
            P("seq", None),
            P("seq", None),
            P("seq", None),
            P("seq", None),
            P("exp", None, ("seq", "hid")),
            P("exp", None, ("seq", "hid")),
            P("exp", ("seq", "hid"), None),
        ),
        out_specs=(
            P("exp", None, ("seq", "hid")),
            P("exp", None, ("seq", "hid")),
            P("exp", ("seq", "hid"), None),
            P("seq", "hid"),
            P("seq", None),
        ),
        check_vma=False,
    )
```

profile of v0, /device:TPU:0, one launch (start us, length us, event | category | flops | bytes accessed | tf_op | source)
XLA Modules:
  0.0 344.5 jit_solution(5438517381305366996)
XLA Ops:
  7.3 0.8 broadcast_compare_fusion
  8.0 0.1 copy.22
  8.2 0.1 reshape.70
  8.3 0.3 reduce-window.9
  8.6 0.1 reshape.71
  8.9 0.1 slice_reduce_fusion
  9.3 1.1 convolution_convert_fusion.1
  10.5 2.5 convolution_convert_fusion
  13.1 0.6 dynamic-slice.1
  13.7 0.6 dynamic-slice
  14.9 41.9 %all-gather.3.cloned.1.call-done = bf16[160,6144]{1,0:T(8,128)(2,1)} async-done(((bf16[40,6144]{1,0:T(8,128)(2,1)}), bf16[160,6144]{1,0:T(8,128)(2,1)}) %all-gather.3.cloned.1.call-update) | async-done | bytes 1966096 | tf_op jit(solution)/shard_map/all_gather | solution.py:33
  56.8 7.5 %fusion = f32[160,1024]{1,0:T(8,128)S(1)} fusion(bf16[160,6144]{1,0:T(8,128)(2,1)} %all-gather.3.cloned.1.call-done, bf16[1,6144,1024]{2,1,0:T(8,128)(2,1)} %param.11), kind=kOutput, calls=%fused_computation | convolution fusion | flops 2013265920 | bytes 15204352 | tf_op jit(solution)/shard_map/dot_general | solution.py:42
  64.4 7.1 %fusion.2 = f32[160,1024]{1,0:T(8,128)S(1)} fusion(bf16[160,6144]{1,0:T(8,128)(2,1)S(1)} %copy-done.2, bf16[1,6144,1024]{2,1,0:T(8,128)(2,1)} %param.12), kind=kOutput, calls=%fused_computation.2 | convolution fusion | flops 2013265920 | bytes 15204352 | tf_op jit(solution)/shard_map/dot_general | solution.py:43
  71.5 29.9 %all-gather.5.cloned.1.call-done = bf16[160,6144]{1,0:T(8,128)(2,1)} async-done(((bf16[40,6144]{1,0:T(8,128)(2,1)}), bf16[160,6144]{1,0:T(8,128)(2,1)}) %all-gather.5.cloned.1.call-update) | async-done | bytes 1966096 | tf_op jit(solution)/shard_map/all_gather | solution.py:34
  101.4 10.4 %fusion.7 = (f32[160]{0:T(256)S(1)}, bf16[160,1024]{1,0:T(8,128)(2,1)}, f32[160,1024]{1,0:T(8,128)}) fusion(f32[160,1024]{1,0:T(8,128)S(1)} %fusion.2, f32[160,1024]{1,0:T(8,128)S(1)} %fusion, bf16[160,6144]{1,0:T(8,128)(2,1)} %all-gather.5.cloned.1.call-done, bf16[1,1024,6144]{2,1,0:T(8,128)(2,1)} %param.13), kind=kOutput, calls=%fused_computation.16 | convolution fusion | flops 2014740352 | bytes 16843392 | tf_op jit(solution)/shard_map/dot_general | solution.py:47
  111.9 40.0 %all-reduce.1 = f32[16,40]{1,0:T(8,128)S(1)} all-reduce(f32[16,40]{1,0:T(8,128)S(1)} %bitcast.64), channel_id=3, replica_groups=mesh['seq'=4,'exp'=2,'hid'=4] {'seq','hid'}, use_global_device_ids=true, to_apply=%region_7.8.clone | all-reduce | flops 640 | bytes 5120
  151.9 0.7 dynamic-slice_bitcast_fusion
  152.6 0.1 select_reduce_fusion
  152.7 0.2 dynamic-update-slice
  153.0 8.5 %all-reduce = bf16[160]{0:T(256)(128)(2,1)S(1)} all-reduce(bf16[160]{0:T(256)(128)(2,1)S(1)} %dynamic-update-slice), channel_id=1, replica_groups=mesh['seq'=4,'exp'=2,'hid'=4] {'seq'}, use_global_device_ids=true, to_apply=%add | all-reduce | flops 160 | bytes 640
  161.5 1.4 multiply_convert_fusion.1
  163.0 9.0 %fusion.15 = f32[4,40,4,1536]{3,1,2,0:T(8,128)S(1)} fusion(bf16[4,40,1024,1]{2,1,3,0:T(8,128)(2,1)S(1)} %bitcast.62, bf16[4,1536,1024,1]{2,1,0,3:T(8,128)(2,1)} %bitcast.59), kind=kOutput, calls=%fused_computation.36 | convolution fusion | flops 2013265920 | bytes 16842752 | tf_op jit(solution)/shard_map/sqf,hcf->shqc/dot_general | solution.py:68
  172.0 10.8 %convolution_add_fusion = f32[4,40,4,1536]{3,1,2,0:T(8,128)} fusion(f32[4,40,4,1536]{3,1,2,0:T(8,128)S(1)} %fusion.15, bf16[4,40,1024,1]{2,1,3,0:T(8,128)(2,1)S(1)} %bitcast.63, bf16[4,1536,1024,1]{2,1,0,3:T(8,128)(2,1)} %bitcast.60), kind=kOutput, calls=%fused_computation.11 | convolution fusion | flops 2014248960 | bytes 20774912 | tf_op jit(solution)/shard_map/sqf,hcf->shqc/dot_general | solution.py:74
  182.9 2.7 psum.15
  185.6 0.6 convert_element_type.76
  186.2 6.6 %convert_bitcast_fusion.1 = bf16[1,6144,1024]{2,1,0:T(8,128)(2,1)} fusion(bf16[160,6144]{1,0:T(8,128)(2,1)S(1)} %copy-done.2, bf16[160,1024]{1,0:T(8,128)(2,1)S(1)} %copy-done.8), kind=kOutput, calls=%fused_computation.7 | convolution fusion | flops 2019557376 | bytes 14876672 | tf_op jit(solution)/shard_map/dot_general | solution.py:63
  192.8 6.6 %convert_bitcast_fusion.2 = bf16[1,6144,1024]{2,1,0:T(8,128)(2,1)} fusion(bf16[160,6144]{1,0:T(8,128)(2,1)S(1)} %copy-done.2, bf16[160,1024]{1,0:T(8,128)(2,1)S(1)} %copy-done.6), kind=kOutput, calls=%fused_computation.8 | convolution fusion | flops 2019557376 | bytes 14876672 | tf_op jit(solution)/shard_map/dot_general | solution.py:60
  199.4 116.0 %reduce-scatter.2.cloned.1.call-done = f32[1,40,1536]{2,1,0:T(8,128)} async-done(((f32[16,40,1536]{2,1,0:T(8,128)}), f32[1,40,1536]{2,1,0:T(8,128)}) %reduce-scatter.2.cloned.1.call-update) | async-done | bytes 245776 | tf_op jit(solution)/shard_map/reduce_scatter | solution.py:86
  315.5 2.5 convolution_convert_fusion.2
  318.0 10.1 %convert_bitcast_fusion = bf16[1,1024,6144]{2,1,0:T(8,128)(2,1)} fusion(bf16[160,6144]{1,0:T(8,128)(2,1)} %all-gather.5.cloned.1.call-done, bf16[160,1024]{1,0:T(8,128)(2,1)} %get-tuple-element.8, f32[160]{0:T(256)S(1)} %convert_element_type.63), kind=kOutput, calls=%fused_computation.6 | convolution fusion | flops 2020048896 | bytes 14877312 | tf_op jit(solution)/shard_map/dot_general | solution.py:52
  328.1 7.9 %all-reduce.4.cloned.1.call-done = bf16[128,1536]{1,0:T(8,128)(2,1)} async-done(((bf16[128,1536]{1,0:T(8,128)(2,1)}), bf16[128,1536]{1,0:T(8,128)(2,1)}) %all-reduce.4.cloned.1.call-update) | async-done | bytes 393232 | tf_op jit(solution)/shard_map/psum | solution.py:96
  336.1 2.0 convert_element_type.74
  (43 shorter events, 0.7 us)
Async XLA Ops:
  7.2 2.1 copy-start
  7.2 5.9 %copy-start.11 = (u32[32]{0:T(128)S(1)}, u32[32]{0:T(128)}, u32[]{:S(2)}) copy-start(u32[32]{0:T(128)} %constant.32) | copy-start | bytes 388
  7.2 6.5 %copy-start.10 = (u32[32]{0:T(128)S(1)}, u32[32]{0:T(128)}, u32[]{:S(2)}) copy-start(u32[32]{0:T(128)} %constant.26) | copy-start | bytes 388
  7.2 49.6 %all-gather.3.cloned.1.call-start = ((), (), s32[]{:S(2)}) async-start(), calls=%async_computation.1 | async-start | bytes 2457600 | tf_op jit(solution)/shard_map/all_gather | solution.py:33
  9.3 5.7 %copy-start.3 = (f32[128,40]{0,1:T(8,128)}, f32[128,40]{0,1:T(8,128)S(1)}, u32[]{:S(2)}) copy-start(f32[128,40]{0,1:T(8,128)S(1)} %convert_reduce_fusion) | copy-start | bytes 61444
  10.4 91.0 %all-gather.5.cloned.1.call-start = ((), (), s32[]{:S(2)}) async-start(), calls=%async_computation.2 | async-start | bytes 2457600 | tf_op jit(solution)/shard_map/all_gather | solution.py:34
  13.0 302.4 %reduce-scatter.2.cloned.1.call-start = ((), (), s32[]{:S(2)}) async-start(), calls=%async_computation.3 | async-start | bytes 4177920 | tf_op jit(solution)/shard_map/reduce_scatter | solution.py:86
  56.8 7.5 %copy-start.2 = (bf16[160,6144]{1,0:T(8,128)(2,1)S(1)}, bf16[160,6144]{1,0:T(8,128)(2,1)}, u32[]{:S(2)}) copy-start(bf16[160,6144]{1,0:T(8,128)(2,1)} %all-gather.3.cloned.1.call-done) | copy-start | bytes 5898244
  71.5 81.1 %copy-start.9 = (f32[128,2]{0,1:T(2,128)S(1)}, f32[128,2]{0,1:T(2,128)}, u32[]{:S(2)}) copy-start(f32[128,2]{0,1:T(2,128)} %param.10) | copy-start | bytes 3076
  163.0 9.0 %copy-start.5 = (bf16[160,1024]{1,0:T(8,128)(2,1)}, bf16[160,1024]{1,0:T(8,128)(2,1)S(1)}, u32[]{:S(2)}) copy-start(bf16[160,1024]{1,0:T(8,128)(2,1)S(1)} %get-tuple-element.12) | copy-start | bytes 983044
  163.0 9.0 %copy-start.7 = (bf16[160,1024]{1,0:T(8,128)(2,1)}, bf16[160,1024]{1,0:T(8,128)(2,1)S(1)}, u32[]{:S(2)}) copy-start(bf16[160,1024]{1,0:T(8,128)(2,1)S(1)} %get-tuple-element.11) | copy-start | bytes 983044
  182.8 3.3 copy-start.8
  182.8 153.2 %all-reduce.4.cloned.1.call-start = ((), (), s32[]{:S(2)}) async-start(), calls=%async_computation.4 | async-start | bytes 786432 | tf_op jit(solution)/shard_map/psum | solution.py:96
  186.2 6.6 %copy-start.6 = (bf16[160,1024]{1,0:T(8,128)(2,1)S(1)}, bf16[160,1024]{1,0:T(8,128)(2,1)}, u32[]{:S(2)}) copy-start(bf16[160,1024]{1,0:T(8,128)(2,1)} %copy-done.5) | copy-start | bytes 983044
  192.8 122.7 %copy-start.4 = (f32[128,40]{0,1:T(8,128)S(1)}, f32[128,40]{0,1:T(8,128)}, u32[]{:S(2)}) copy-start(f32[128,40]{0,1:T(8,128)} %copy-done.3) | copy-start | bytes 61444
  318.0 20.0 %copy-start.1 = (bf16[128,6144]{1,0:T(8,128)(2,1)S(1)}, bf16[128,6144]{1,0:T(8,128)(2,1)}, u32[]{:S(2)}) copy-start(bf16[128,6144]{1,0:T(8,128)(2,1)} %param.7) | copy-start | bytes 4718596
Sparse Core Ops, SparseCore 0:
  10.5 46.2 all-gather.2
  59.0 42.3 all-gather.4
  183.0 132.4 reduce-scatter.1
  318.2 17.7 all-reduce.3
where the time goes:
time: 345 us
  waiting for transfers between devices  196 us (57%)
  matrix products  74.3 us (22%)
  blocking collectives  51.3 us (15%)
  between operations  14.6 us (4%)
  other arithmetic  5.25 us (2%)
    reduce_scatter x1, waiting for transfers between devices, on_device(): lax.psum_scatter(flat_parts, ('seq', 'hid'), scatter_dimension=0, tiled=T...  116 us
    unnamed x2, blocking collectives  48.6 us
    all_gather x1, waiting for transfers between devices, on_device(): lax.all_gather(token_slots, 'seq', axis=0, tiled=True)  41.9 us
    all_gather x1, waiting for transfers between devices, on_device(): lax.all_gather(grad_slots, 'seq', axis=0, tiled=True)  29.9 us
    dot_general x1, matrix products, on_device(): jnp.einsum('sqf,hcf->shqc', up_blocks, up_mat.reshape(hid_count, piece_wi...  10.8 us
    dot_general x1, matrix products, on_device(): lax.dot_general(grads_e, down_mat, (((1,), (1,)), ((), ())), preferred_el...  10.4 us
    dot_general x1, matrix products, on_device(): lax.dot_general(weighted, grads_e, contract_rows, preferred_element_type=...  10.1 us
    dot_general x1, matrix products, on_device(): jnp.einsum('sqf,hcf->shqc', gate_blocks, gate_mat.reshape(hid_count, piec...  9.01 us
  transfers between devices with their start and end apart: 4, of which 4 were waited for; matrix products, arithmetic and copies ran while one was open for 12% of the time, Pallas kernels for 0%

commit v1 on v0

--- a/solution.py
+++ b/solution.py
@@ -93,7 +93,7 @@
     )
     gate_part = jnp.sum(pick_table * slot_grad[None, None, :], axis=2)
     token_sum, gate_sum = (
-        lax.psum(token_part.astype(jnp.bfloat16), "exp").astype(jnp.float32),
+        jnp.sum(lax.all_gather(token_part.astype(jnp.bfloat16), "exp"), axis=0).astype(jnp.float32),
         lax.psum(gate_part.astype(jnp.bfloat16), "exp").astype(jnp.float32),
     )
     return (grad_gate[None], grad_up[None], grad_down[None], token_sum, gate_sum)

time: 345 us -> 328 us (0.951)
  waiting for transfers between devices: 196 us -> 179 us
    reduce_scatter x1, waiting for transfers between devices: 116 us -> 108 us  [on_device(): lax.psum_scatter(flat_parts, ('seq', 'hid'), scatter_dimension=0, tiled=T...]
    psum x1 -> x0, waiting for transfers between devices: 7.95 us -> none  [on_device(): lax.psum(token_part.astype(jnp.bfloat16), 'exp').astype(jnp.float32)]
  transfers between devices with their start and end apart: 4 -> 3, of which waited for: 4 -> 3; matrix products, arithmetic and copies ran while one was open for 12% -> 12% of each run, Pallas kernels for 0% -> 0%
where the time goes in v1:
time: 328 us; the launch traced here: 327 us
  waiting for transfers between devices  179 us (55%)
  matrix products  71.7 us (22%)
  blocking collectives  53.8 us (16%)
  between operations  14.6 us (4%)
  other arithmetic  4.42 us (1%)
    reduce_scatter x1, waiting for transfers between devices, on_device(): lax.psum_scatter(flat_parts, ('seq', 'hid'), scatter_dimension=0, tiled=T...  108 us
    unnamed x2, blocking collectives  48.6 us
    all_gather x1, waiting for transfers between devices, on_device(): lax.all_gather(token_slots, 'seq', axis=0, tiled=True)  41.9 us
    all_gather x1, waiting for transfers between devices, on_device(): lax.all_gather(grad_slots, 'seq', axis=0, tiled=True)  29.9 us
    dot_general x1, matrix products, on_device(): jnp.einsum('sqf,hcf->shqc', up_blocks, up_mat.reshape(hid_count, piece_wi...  10.8 us
    dot_general x1, matrix products, on_device(): lax.dot_general(grads_e, down_mat, (((1,), (1,)), ((), ())), preferred_el...  10.4 us
    dot_general x1, matrix products, on_device(): jnp.einsum('sqf,hcf->shqc', gate_blocks, gate_mat.reshape(hid_count, piec...  9.01 us
    dot_general x1, matrix products, on_device(): lax.dot_general(weighted, grads_e, contract_rows, preferred_element_type=...  8.28 us
  transfers between devices with their start and end apart: 3, of which 3 were waited for; matrix products, arithmetic and copies ran while one was open for 12% of the time, Pallas kernels for 0%

profile of v1, /device:TPU:0, one launch (start us, length us, event | category | flops | bytes accessed | tf_op | source)
XLA Modules:
  0.0 327.1 jit_solution(12092087766518935879)
XLA Ops:
  7.3 0.8 broadcast_compare_fusion
  8.2 0.1 reshape.70
  8.3 0.3 reduce-window.9
  8.6 0.1 reshape.71
  8.9 0.1 slice_reduce_fusion
  9.3 1.1 convolution_convert_fusion.1
  10.5 2.5 convolution_convert_fusion
  13.1 0.6 dynamic-slice.1
  13.7 0.6 dynamic-slice
  14.9 41.9 %all-gather.4.cloned.1.call-done = bf16[160,6144]{1,0:T(8,128)(2,1)} async-done(((bf16[40,6144]{1,0:T(8,128)(2,1)}), bf16[160,6144]{1,0:T(8,128)(2,1)}) %all-gather.4.cloned.1.call-update) | async-done | bytes 1966096 | tf_op jit(solution)/shard_map/all_gather | solution.py:33
  56.8 7.5 %fusion = f32[160,1024]{1,0:T(8,128)S(1)} fusion(bf16[160,6144]{1,0:T(8,128)(2,1)} %all-gather.4.cloned.1.call-done, bf16[1,6144,1024]{2,1,0:T(8,128)(2,1)} %param.11), kind=kOutput, calls=%fused_computation | convolution fusion | flops 2013265920 | bytes 15204352 | tf_op jit(solution)/shard_map/dot_general | solution.py:42
  64.4 7.1 %fusion.2 = f32[160,1024]{1,0:T(8,128)S(1)} fusion(bf16[160,6144]{1,0:T(8,128)(2,1)S(1)} %copy-done.2, bf16[1,6144,1024]{2,1,0:T(8,128)(2,1)} %param.12), kind=kOutput, calls=%fused_computation.2 | convolution fusion | flops 2013265920 | bytes 15204352 | tf_op jit(solution)/shard_map/dot_general | solution.py:43
  71.5 29.9 %all-gather.6.cloned.1.call-done = bf16[160,6144]{1,0:T(8,128)(2,1)} async-done(((bf16[40,6144]{1,0:T(8,128)(2,1)}), bf16[160,6144]{1,0:T(8,128)(2,1)}) %all-gather.6.cloned.1.call-update) | async-done | bytes 1966096 | tf_op jit(solution)/shard_map/all_gather | solution.py:34
  101.4 10.4 %fusion.7 = (f32[160]{0:T(256)S(1)}, bf16[160,1024]{1,0:T(8,128)(2,1)}, f32[160,1024]{1,0:T(8,128)}) fusion(f32[160,1024]{1,0:T(8,128)S(1)} %fusion.2, f32[160,1024]{1,0:T(8,128)S(1)} %fusion, bf16[160,6144]{1,0:T(8,128)(2,1)} %all-gather.6.cloned.1.call-done, bf16[1,1024,6144]{2,1,0:T(8,128)(2,1)} %param.13), kind=kOutput, calls=%fused_computation.16 | convolution fusion | flops 2014740352 | bytes 16843392 | tf_op jit(solution)/shard_map/dot_general | solution.py:47
  111.9 40.0 %all-reduce.1 = f32[16,40]{1,0:T(8,128)S(1)} all-reduce(f32[16,40]{1,0:T(8,128)S(1)} %bitcast.66), channel_id=4, replica_groups=mesh['seq'=4,'exp'=2,'hid'=4] {'seq','hid'}, use_global_device_ids=true, to_apply=%region_7.8.clone | all-reduce | flops 640 | bytes 5120
  151.9 0.7 dynamic-slice_bitcast_fusion
  152.6 0.1 select_reduce_fusion
  152.7 0.2 dynamic-update-slice
  153.0 8.5 %all-reduce = bf16[160]{0:T(256)(128)(2,1)S(1)} all-reduce(bf16[160]{0:T(256)(128)(2,1)S(1)} %dynamic-update-slice), channel_id=1, replica_groups=mesh['seq'=4,'exp'=2,'hid'=4] {'seq'}, use_global_device_ids=true, to_apply=%add | all-reduce | flops 160 | bytes 640
  161.5 1.4 multiply_convert_fusion.1
  163.0 9.0 %fusion.15 = f32[4,40,4,1536]{3,1,2,0:T(8,128)S(1)} fusion(bf16[4,40,1024,1]{2,1,3,0:T(8,128)(2,1)S(1)} %bitcast.64, bf16[4,1536,1024,1]{2,1,0,3:T(8,128)(2,1)} %bitcast.60), kind=kOutput, calls=%fused_computation.36 | convolution fusion | flops 2013265920 | bytes 16842752 | tf_op jit(solution)/shard_map/sqf,hcf->shqc/dot_general | solution.py:68
  172.0 10.8 %convolution_add_fusion = f32[4,40,4,1536]{3,1,2,0:T(8,128)} fusion(f32[4,40,4,1536]{3,1,2,0:T(8,128)S(1)} %fusion.15, bf16[4,40,1024,1]{2,1,3,0:T(8,128)(2,1)S(1)} %bitcast.65, bf16[4,1536,1024,1]{2,1,0,3:T(8,128)(2,1)} %bitcast.61), kind=kOutput, calls=%fused_computation.11 | convolution fusion | flops 2014248960 | bytes 20774912 | tf_op jit(solution)/shard_map/sqf,hcf->shqc/dot_general | solution.py:74
  182.8 2.8 psum.7
  185.6 0.6 convert_element_type.78
  186.2 8.3 %convert_bitcast_fusion = bf16[1,1024,6144]{2,1,0:T(8,128)(2,1)} fusion(bf16[160,6144]{1,0:T(8,128)(2,1)} %all-gather.6.cloned.1.call-done, bf16[160,1024]{1,0:T(8,128)(2,1)S(1)} %copy-done.8, f32[160]{0:T(256)S(1)} %convert_element_type.65), kind=kOutput, calls=%fused_computation.6 | convolution fusion | flops 2020048896 | bytes 14877312 | tf_op jit(solution)/shard_map/dot_general | solution.py:52
  194.5 6.6 %convert_bitcast_fusion.1 = bf16[1,6144,1024]{2,1,0:T(8,128)(2,1)} fusion(bf16[160,6144]{1,0:T(8,128)(2,1)S(1)} %copy-done.2, bf16[160,1024]{1,0:T(8,128)(2,1)S(1)} %copy-done.7), kind=kOutput, calls=%fused_computation.7 | convolution fusion | flops 2019557376 | bytes 14876672 | tf_op jit(solution)/shard_map/dot_general | solution.py:63
  201.1 6.6 %convert_bitcast_fusion.2 = bf16[1,6144,1024]{2,1,0:T(8,128)(2,1)} fusion(bf16[160,6144]{1,0:T(8,128)(2,1)S(1)} %copy-done.2, bf16[160,1024]{1,0:T(8,128)(2,1)S(1)} %copy-done.5), kind=kOutput, calls=%fused_computation.8 | convolution fusion | flops 2019557376 | bytes 14876672 | tf_op jit(solution)/shard_map/dot_general | solution.py:60
  207.7 107.5 %reduce-scatter.2.cloned.1.call-done = f32[1,40,1536]{2,1,0:T(8,128)} async-done(((f32[16,40,1536]{2,1,0:T(8,128)}), f32[1,40,1536]{2,1,0:T(8,128)}) %reduce-scatter.2.cloned.1.call-update) | async-done | bytes 245776 | tf_op jit(solution)/shard_map/reduce_scatter | solution.py:86
  315.3 1.8 convolution_convert_fusion.2
  317.1 2.4 all-gather
  319.4 0.2 reduce_sum.50
  319.6 1.0 convert_element_type.76
  (42 shorter events, 0.8 us)
Async XLA Ops:
  7.2 2.1 copy-start
  7.2 5.9 %copy-start.11 = (u32[32]{0:T(128)S(1)}, u32[32]{0:T(128)}, u32[]{:S(2)}) copy-start(u32[32]{0:T(128)} %constant.34) | copy-start | bytes 388
  7.2 6.5 %copy-start.10 = (u32[32]{0:T(128)S(1)}, u32[32]{0:T(128)}, u32[]{:S(2)}) copy-start(u32[32]{0:T(128)} %constant.28) | copy-start | bytes 388
  7.2 49.6 %all-gather.4.cloned.1.call-start = ((), (), s32[]{:S(2)}) async-start(), calls=%async_computation.1 | async-start | bytes 2457600 | tf_op jit(solution)/shard_map/all_gather | solution.py:33
  9.3 5.7 %copy-start.3 = (f32[128,40]{0,1:T(8,128)}, f32[128,40]{0,1:T(8,128)S(1)}, u32[]{:S(2)}) copy-start(f32[128,40]{0,1:T(8,128)S(1)} %convert_reduce_fusion) | copy-start | bytes 61444
  10.4 91.0 %all-gather.6.cloned.1.call-start = ((), (), s32[]{:S(2)}) async-start(), calls=%async_computation.2 | async-start | bytes 2457600 | tf_op jit(solution)/shard_map/all_gather | solution.py:34
  13.0 302.3 %reduce-scatter.2.cloned.1.call-start = ((), (), s32[]{:S(2)}) async-start(), calls=%async_computation.3 | async-start | bytes 4177920 | tf_op jit(solution)/shard_map/reduce_scatter | solution.py:86
  56.8 7.5 %copy-start.2 = (bf16[160,6144]{1,0:T(8,128)(2,1)S(1)}, bf16[160,6144]{1,0:T(8,128)(2,1)}, u32[]{:S(2)}) copy-start(bf16[160,6144]{1,0:T(8,128)(2,1)} %all-gather.4.cloned.1.call-done) | copy-start | bytes 5898244
  71.5 81.1 %copy-start.9 = (f32[128,2]{0,1:T(2,128)S(1)}, f32[128,2]{0,1:T(2,128)}, u32[]{:S(2)}) copy-start(f32[128,2]{0,1:T(2,128)} %param.10) | copy-start | bytes 3076
  163.0 9.0 %copy-start.4 = (bf16[160,1024]{1,0:T(8,128)(2,1)}, bf16[160,1024]{1,0:T(8,128)(2,1)S(1)}, u32[]{:S(2)}) copy-start(bf16[160,1024]{1,0:T(8,128)(2,1)S(1)} %get-tuple-element.12) | copy-start | bytes 983044
  163.0 9.0 %copy-start.6 = (bf16[160,1024]{1,0:T(8,128)(2,1)}, bf16[160,1024]{1,0:T(8,128)(2,1)S(1)}, u32[]{:S(2)}) copy-start(bf16[160,1024]{1,0:T(8,128)(2,1)S(1)} %get-tuple-element.11) | copy-start | bytes 983044
  182.8 3.4 %copy-start.8 = (bf16[160,1024]{1,0:T(8,128)(2,1)S(1)}, bf16[160,1024]{1,0:T(8,128)(2,1)}, u32[]{:S(2)}) copy-start(bf16[160,1024]{1,0:T(8,128)(2,1)} %get-tuple-element.8) | copy-start | bytes 983044
  186.2 8.3 %copy-start.7 = (bf16[160,1024]{1,0:T(8,128)(2,1)S(1)}, bf16[160,1024]{1,0:T(8,128)(2,1)}, u32[]{:S(2)}) copy-start(bf16[160,1024]{1,0:T(8,128)(2,1)} %copy-done.6) | copy-start | bytes 983044
  194.5 6.6 %copy-start.5 = (bf16[160,1024]{1,0:T(8,128)(2,1)S(1)}, bf16[160,1024]{1,0:T(8,128)(2,1)}, u32[]{:S(2)}) copy-start(bf16[160,1024]{1,0:T(8,128)(2,1)} %copy-done.4) | copy-start | bytes 983044
  201.1 119.5 %copy-start.1 = (bf16[128,6144]{1,0:T(8,128)(2,1)S(1)}, bf16[128,6144]{1,0:T(8,128)(2,1)}, u32[]{:S(2)}) copy-start(bf16[128,6144]{1,0:T(8,128)(2,1)} %param.7) | copy-start | bytes 4718596
Sparse Core Ops, SparseCore 0:
  10.5 46.2 all-gather.3
  59.0 42.3 all-gather.5
  182.9 132.3 reduce-scatter.1
